TPU v7x, 32 devices: a whole 2x2x4 slice. The times are simulated.
32 devices in a mesh: parts: 2 (over x), col: 16 (over z, y, core).
Axes of the slice: x: 2, y: 2, z: 4, core: 2. Of those that a mesh axis runs over, the one named last changes fastest.
Arguments:
- view_factors: bfloat16 [8192, 4096], P(('parts', 'col')), parts along dimension 0, may hold values from -0.09375 to 0.09375
- direct_coeff: bfloat16 [8192, 2304], P(('parts', 'col')), parts along dimension 0, may hold values from -6 to 6
- material: int32 [8192], P(('parts', 'col')), parts along dimension 0, may hold values from 0 to 15
- albedo: float32 [32], P('parts'), parts along dimension 0, may hold values from 0.1 to 0.9
- sky_matrix: bfloat16 [2304, 128], P('col'), may hold values from -0.125 to 0.125
- sky_order: int32 [2304], replicated, may hold values from 0 to 2303, each once
Outputs:
- irradiance: bfloat16 [8192, 128], P(('parts', 'col')), parts along dimension 0
There are 2 independent parts, one for each index of `parts`. A program takes and returns all parts, laid end to end along the dimension named above; an argument that names none is the same for every part. Nothing has to cross between parts.
Inputs may be any that keep to these rules, and one draw needn't show every extreme that they name: sky_order names each of 0 to 2303 once.
All inputs are finite; a program needn't handle non-finite values.
Results may differ from a plain program's by a relative error of at most 0.0055.
Values may be sent and summed in bfloat16 or wider, within the bound.
A program may use at most 128 MiB of HBM per device.

v0:
```python
import jax
import jax.numpy as jnp
from jax import lax
from jax.sharding import PartitionSpec as P


def split_parts(values):
    upper = values.astype(jnp.bfloat16)
    lower = (values - upper.astype(jnp.float32)).astype(jnp.bfloat16)
    return (upper, lower)


def shards(view_factors, direct_coeff, material, albedo, sky_matrix, sky_order):
    inverse = jnp.argsort(sky_order)
    direct_sorted = jnp.take(direct_coeff, inverse, axis=1)
    matches = material[:, None] == jnp.arange(albedo.shape[0], dtype=jnp.int32)[None, :]
    reflectance = jnp.sum(jnp.where(matches, albedo[None, :], 0.0), axis=1)
    reflected = (reflectance[:, None] * direct_sorted.astype(jnp.float32)).astype(jnp.bfloat16)
    piece = lax.all_gather(sky_matrix, "col", axis=0, tiled=True)
    direct_hours = jnp.dot(direct_sorted, piece, preferred_element_type=jnp.float32)
    own_reflected = jnp.dot(reflected, piece, preferred_element_type=jnp.float32)
    upper, lower = split_parts(lax.all_gather(own_reflected, "col", axis=0, tiled=True))
    running = jnp.dot(view_factors, upper, preferred_element_type=jnp.float32)
    bounce_hours = running + jnp.dot(view_factors, lower, preferred_element_type=jnp.float32)
    irradiance = direct_hours + bounce_hours
    return irradiance.astype(jnp.bfloat16)


def solution(mesh):
    return jax.shard_map(
        shards,
        mesh=mesh,
        in_specs=(
            P(("parts", "col"), None),
            P(("parts", "col"), None),
            P(("parts", "col")),
            P("parts"),
            P("col", None),
            P(),
        ),
        out_specs=P(("parts", "col"), None),
        check_vma=False,
    )
```

profile of v0, /device:TPU:0, one launch (start us, length us, event | category | flops | bytes accessed | tf_op | source)
XLA Modules:
  0.0 101.5 jit_solution(16061025368571012396)
XLA Ops:
  6.5 0.0 copy-start
  6.5 0.0 all-gather.2.cloned.1.call-start
  6.5 6.6 %sort.17 = (s32[2304]{0:T(1024)}, s32[2304]{0:T(1024)S(1)}) sort(s32[2304]{0:T(1024)} %param.11, s32[2304]{0:T(1024)S(1)} %iota.8), dimensions={0}, to_apply=%region_0.0 | sort | flops 27648 | bytes 36864 | tf_op jit(solution)/shard_map/jit(argsort)/sort | solution.py:14
  13.2 26.5 %all_gather.6 = bf16[2304,128]{1,0:T(8,128)(2,1)} all-gather(bf16[144,128]{1,0:T(8,128)(2,1)} %param.10), channel_id=1, replica_groups=mesh['parts'=2,'col'=16] {'col'}, dimensions={0}, use_global_device_ids=true | all-gather | bytes 626688 | tf_op jit(solution)/shard_map/all_gather | solution.py:19
  39.7 0.0 copy-start.3
  39.7 0.0 copy-start.4
  39.7 1.6 %copy.10 = bf16[256,2304]{0,1:T(8,128)(2,1)S(1)} copy(bf16[256,2304]{1,0:T(8,128)(2,1)} %param.7) | data formatting | bytes 2359296 | tf_op args[1]
  41.3 0.0 copy-done.3
  41.3 0.0 copy-done.4
  41.3 0.1 select_reduce_fusion
  41.4 7.4 %gather_fusion = bf16[2304,256]{1,0:T(8,128)(2,1)} fusion(bf16[256,2304]{0,1:T(8,128)(2,1)S(1)} %copy.10, s32[3072]{0:T(1024)S(1)} %pad_clamp_fusion), kind=kCustom, calls=%fused_computation | custom fusion | bytes 2368512 | tf_op jit(solution)/shard_map/jit(_take)/gather | solution.py:15
  48.9 0.0 copy-start.2
  48.9 3.1 %fusion = f32[256,128]{1,0:T(8,128)} fusion(bf16[2304,128]{1,0:T(8,128)(2,1)} %all_gather.6, f32[256]{0:T(256)S(1)} %select_reduce_fusion, bf16[2304,256]{1,0:T(8,128)(2,1)} %gather_fusion, pred[2304]{0:T(1024)(128)(4,1)S(1)} %compare_and_fusion), kind=kOutput, calls=%fused_computation.3 | convolution fusion | flops 153354240 | bytes 1903872 | tf_op jit(solution)/shard_map/dot_general | solution.py:21
  51.9 0.0 all-gather.2.cloned.1.call-update
  52.0 0.0 copy-done.2
  52.0 1.9 %fusion.8 = f32[256,128]{1,0:T(8,128)S(1)} fusion(bf16[2304,128]{1,0:T(8,128)(2,1)} %all_gather.6, bf16[2304,256]{1,0:T(8,128)(2,1)S(1)} %copy-done.2, pred[2304]{0:T(1024)(128)(4,1)S(1)} %compare_and_fusion), kind=kOutput, calls=%fused_computation.13 | convolution fusion | flops 151584768 | bytes 1902848 | tf_op jit(solution)/shard_map/dot_general | solution.py:20
  53.9 36.9 %all-gather.2.cloned.1.call-done = f32[4096,128]{1,0:T(8,128)} async-done(((f32[256,128]{1,0:T(8,128)}), f32[4096,128]{1,0:T(8,128)}) %all-gather.2.cloned.1.call-update) | async-done | bytes 2097168 | tf_op jit(solution)/shard_map/all_gather | solution.py:22
  90.8 0.0 copy-done
  90.8 0.0 copy-start.1
  90.8 2.4 %fusion.6 = f32[128,256]{0,1:T(8,128)S(1)} fusion(bf16[256,4096]{1,0:T(8,128)(2,1)S(1)} %copy-done, f32[4096,128]{1,0:T(8,128)} %all-gather.2.cloned.1.call-done), kind=kOutput, calls=%fused_computation.11 | convolution fusion | flops 268959744 | bytes 4325376 | tf_op jit(solution)/shard_map/dot_general | solution.py:23
  93.3 0.0 copy-done.1
  93.3 1.3 %fusion.4 = bf16[256,128]{1,0:T(8,128)(2,1)} fusion(f32[256,128]{1,0:T(8,128)S(1)} %fusion.8, f32[128,256]{0,1:T(8,128)S(1)} %fusion.6, bf16[256,4096]{1,0:T(8,128)(2,1)S(1)} %copy-done, f32[4096,128]{1,0:T(8,128)S(1)} %copy-done.1), kind=kOutput, calls=%fused_computation.9 | convolution fusion | flops 270630912 | bytes 4521984 | tf_op jit(solution)/shard_map/dot_general | solution.py:24
  (4 shorter events, 0.0 us)
Async XLA Ops:
  6.5 84.3 %copy-start = (bf16[256,4096]{1,0:T(8,128)(2,1)S(1)}, bf16[256,4096]{1,0:T(8,128)(2,1)}, u32[]{:S(2)}) copy-start(bf16[256,4096]{1,0:T(8,128)(2,1)} %param.6) | copy-start | bytes 6291460
  6.5 84.3 %all-gather.2.cloned.1.call-start = ((), (), s32[]{:S(2)}) async-start(), calls=%async_computation | async-start | bytes 2228224 | tf_op jit(solution)/shard_map/all_gather | solution.py:22
  39.7 1.6 %copy-start.3 = (s32[256]{0:T(256)S(1)}, s32[256]{0:T(256)}, u32[]{:S(2)}) copy-start(s32[256]{0:T(256)} %param.8) | copy-start | bytes 3076
  39.7 1.6 %copy-start.4 = (f32[16]{0:T(128)S(1)}, f32[16]{0:T(128)}, u32[]{:S(2)}) copy-start(f32[16]{0:T(128)} %param.9) | copy-start | bytes 196
  48.9 3.1 %copy-start.2 = (bf16[2304,256]{1,0:T(8,128)(2,1)S(1)}, bf16[2304,256]{1,0:T(8,128)(2,1)}, u32[]{:S(2)}) copy-start(bf16[2304,256]{1,0:T(8,128)(2,1)} %gather_fusion) | copy-start | bytes 3538948
  90.8 2.4 %copy-start.1 = (f32[4096,128]{1,0:T(8,128)S(1)}, f32[4096,128]{1,0:T(8,128)}, u32[]{:S(2)}) copy-start(f32[4096,128]{1,0:T(8,128)} %all-gather.2.cloned.1.call-done) | copy-start | bytes 6291460
Sparse Core Ops, SparseCore 0:
  52.1 38.6 all-gather.1
where the time goes:
time: 102 us; the launch traced here: 101 us
  waiting for transfers between devices  36.9 us (36%)
  blocking collectives  26.5 us (26%)
  between operations  13.5 us (13%)
  local copies, waits for them, and re-layouts  9.05 us (9%)
  matrix products  8.78 us (9%)
  other arithmetic  6.73 us (7%)
    all_gather x1, waiting for transfers between devices, shards(): lax.all_gather(own_reflected, 'col', axis=0, tiled=True)  36.9 us
    all_gather x1, blocking collectives, shards(): piece = lax.all_gather(sky_matrix, 'col', axis=0, tiled=True)  26.5 us
    gather x1, local copies, waits for them, and re-layouts, shards(): direct_sorted = jnp.take(direct_coeff, inverse, axis=1)  7.43 us
    sort x1, other arithmetic, shards(): inverse = jnp.argsort(sky_order)  6.62 us
    dot_general x1, matrix products, shards(): jnp.dot(reflected, piece, preferred_element_type=jnp.float32)  3.06 us
    dot_general x1, matrix products, shards(): running = jnp.dot(view_factors, upper, preferred_element_type=jnp.float32)  2.44 us
  transfers between devices with their start and end apart: 1, of which 1 were waited for; matrix products, arithmetic and copies ran while one was open for 2% of the time, Pallas kernels for 0%

commit v1 on v0

v1 whole, which is shorter than its diff:
```python
import functools

import jax
import jax.numpy as jnp
from jax import lax
from jax.experimental import pallas as pl
from jax.experimental.pallas import tpu as pltpu
from jax.sharding import PartitionSpec as P

MESH = pl.DeviceIdType.MESH
LANES = 128
WIDE = 256
BF16 = jnp.bfloat16
F32 = jnp.float32


def partner(index, step, count):
    if count & (count - 1):
        return lax.rem(index + step, count)
    result, bit = 0, 1
    while bit < count:
        digit = lax.rem(lax.div(index, bit), 2)
        if step & bit:
            digit = 1 - digit
        result = result + digit * bit
        bit *= 2
    return result


def kernel(
    dims,
    view_hbm,
    direct_hbm,
    material_ref,
    albedo_ref,
    sky_hbm,
    place_ref,
    out_ref,
    view_ref,
    direct_ref,
    sky_all,
    hours_all,
    low_ref,
    high_ref,
    reflectance_ref,
    sorted_ref,
    reflected_ref,
    load_sem,
    send_sem,
    recv_sem,
):
    nz, ny, nc = dims
    me = lax.axis_index("col")
    c = lax.rem(me, nc)
    y = lax.rem(lax.div(me, nc), ny)
    z = lax.div(me, nc * ny)

    def index(zz, yy, cc):
        return (zz * ny + yy) * nc + cc

    zs = [partner(z, d, nz) for d in range(nz)]
    zs[0] = z
    line = [index(zz, y, c) for zz in zs[1:]]
    across = index(z, 1 - y, c) if ny == 2 else None
    twin = index(z, y, 1 - c) if nc == 2 else None
    partners = line + [p for p in (across, twin) if p is not None]

    rows = view_ref.shape[0]
    sky_rows = sky_hbm.shape[0]
    own_sky = sky_all.at[pl.ds(pl.multiple_of(me * sky_rows, 16), sky_rows), :]

    load_sky = pltpu.make_async_copy(sky_hbm, own_sky, load_sem.at[0])
    load_direct = pltpu.make_async_copy(direct_hbm, direct_ref, load_sem.at[1])
    load_view = pltpu.make_async_copy(view_hbm, view_ref, load_sem.at[2])
    load_sky.start()
    load_direct.start()
    load_view.start()

    barrier = pltpu.get_barrier_semaphore()
    for p in partners:
        pl.semaphore_signal(barrier, inc=1, device_id={"col": p}, device_id_type=MESH)

    lane = lax.broadcasted_iota(jnp.int32, (LANES, LANES), 1)
    for b in range(place_ref.shape[0]):
        spot = jnp.broadcast_to(place_ref[b : b + 1, :], (LANES, LANES)).T
        low = jnp.where(lax.bitwise_and(spot, LANES - 1) == lane, 1.0, 0.0)
        low_ref[b * LANES : (b + 1) * LANES, :] = low.astype(BF16)
        high = lax.shift_right_logical(spot, LANES.bit_length() - 1)
        high_ref[b * LANES : (b + 1) * LANES, :] = high.astype(F32).astype(BF16)
    for b in range(material_ref.shape[0]):
        kind = jnp.broadcast_to(material_ref[b : b + 1, :], (LANES, LANES)).T
        value = jnp.zeros((LANES, LANES), F32)
        for m in range(albedo_ref.shape[0]):
            value = jnp.where(kind == m, albedo_ref[m], value)
        reflectance_ref[b * LANES : (b + 1) * LANES, :] = value

    load_sky.wait()
    pl.semaphore_wait(barrier, len(partners))

    sends = []

    def send(phase, everyone, block, owner, target, route):
        part = everyone.at[pl.ds(pl.multiple_of(owner * block, 16), block), :]
        copy = pltpu.make_async_remote_copy(
            src_ref=part,
            dst_ref=part,
            send_sem=send_sem.at[phase, route],
            recv_sem=recv_sem.at[phase, owner],
            device_id={"col": target},
            device_id_type=MESH,
        )
        copy.start()
        sends.append(copy)

    def arrived(phase, everyone, block, owner):
        part = everyone.at[pl.ds(pl.multiple_of(owner * block, 16), block), :]
        pltpu.make_async_copy(part, part, recv_sem.at[phase, owner]).wait()

    def gather(phase, everyone, block, work):
        route = iter(range(2 * nz * ny * nc))
        if across is not None:
            send(phase, everyone, block, me, across, next(route))
        for p in reversed(line):
            send(phase, everyone, block, me, p, next(route))
        if twin is not None:
            send(phase, everyone, block, me, twin, next(route))
        work(me)
        waits = []
        for d in range(1, nz):
            waits.append((zs[d], y, True))
        if across is not None:
            waits.insert(0, (z, 1 - y, False))
            for d in range(1, nz):
                waits.append((zs[d], 1 - y, False))
        for zz, yy, forward in waits:
            owner = index(zz, yy, c)
            arrived(phase, everyone, block, owner)
            if forward and across is not None:
                send(phase, everyone, block, owner, across, next(route))
            if twin is not None:
                send(phase, everyone, block, owner, twin, next(route))
            work(owner)
        if twin is not None:
            for zz, yy in [(z, y)] + [(zz, yy) for zz, yy, _ in waits]:
                owner = index(zz, yy, 1 - c)
                arrived(phase, everyone, block, owner)
                work(owner)

    groups = sorted_ref.shape[1] // WIDE
    done = [False]

    def sort_columns(group):
        start = pl.multiple_of(group * WIDE, WIDE)
        halves = []
        for half in range(WIDE // LANES):
            number = (group * (WIDE // LANES) + half).astype(F32).astype(BF16)
            halves.append(jnp.where(high_ref[...] == number, low_ref[...], jnp.zeros((), BF16)))
        chosen = jnp.concatenate(halves, axis=1)
        values = jnp.dot(direct_ref[...], chosen, preferred_element_type=F32)
        sorted_ref[:, pl.ds(start, WIDE)] = values.astype(BF16)
        scale = jnp.concatenate([reflectance_ref[...]] * (WIDE // LANES), axis=1)
        reflected_ref[:, pl.ds(start, WIDE)] = (scale * values).astype(BF16)

    def sort_all(owner):
        if not done[0]:
            done[0] = True
            load_direct.wait()
            lax.fori_loop(0, groups, lambda g, _: (sort_columns(g), 0)[1], 0)

    gather(0, sky_all, sky_rows, sort_all)

    own_hours = pl.ds(pl.multiple_of(me * rows, 16), rows)
    hours_all[own_hours, :] = jnp.dot(reflected_ref[...], sky_all[...], preferred_element_type=F32).astype(BF16)

    total = [None]

    def add(owner):
        if total[0] is None:
            load_view.wait()
            total[0] = jnp.dot(sorted_ref[...], sky_all[...], preferred_element_type=F32)
        start = pl.multiple_of(owner * rows, LANES)
        total[0] = total[0] + jnp.dot(
            view_ref[:, pl.ds(start, rows)], hours_all[pl.ds(start, rows), :], preferred_element_type=F32
        )

    gather(1, hours_all, rows, add)
    out_ref[...] = total[0].astype(out_ref.dtype)
    for copy in sends:
        copy.wait_send()


def shards(dims, view_factors, direct_coeff, material, albedo, sky_matrix, sky_order):
    count = dims[0] * dims[1] * dims[2]
    rows, patches = view_factors.shape
    sky, hours = direct_coeff.shape[1], sky_matrix.shape[1]
    held = sky_matrix.shape[0]
    padded = -(-held // 16) * 16
    place = sky_order
    if padded != held:
        sky_matrix = jnp.pad(sky_matrix, ((0, padded - held), (0, 0)))
        place = sky_order // held * padded + sky_order % held
    width = -(-count * padded // WIDE) * WIDE
    assert width == count * padded and sky % LANES == 0
    routes = 2 * count
    any_spec = pl.BlockSpec(memory_space=pl.ANY)
    vmem = pl.BlockSpec(memory_space=pltpu.VMEM)
    smem = pl.BlockSpec(memory_space=pltpu.SMEM)
    return pl.pallas_call(
        functools.partial(kernel, dims),
        out_shape=jax.ShapeDtypeStruct((rows, hours), BF16),
        in_specs=[any_spec, any_spec, vmem, smem, any_spec, vmem],
        out_specs=vmem,
        scratch_shapes=[
            pltpu.VMEM((rows, patches), BF16),
            pltpu.VMEM((rows, sky), BF16),
            pltpu.VMEM((width, hours), BF16),
            pltpu.VMEM((patches, hours), BF16),
            pltpu.VMEM((sky, LANES), BF16),
            pltpu.VMEM((sky, LANES), BF16),
            pltpu.VMEM((rows, LANES), F32),
            pltpu.VMEM((rows, width), BF16),
            pltpu.VMEM((rows, width), BF16),
            pltpu.SemaphoreType.DMA((3,)),
            pltpu.SemaphoreType.DMA((2, routes)),
            pltpu.SemaphoreType.DMA((2, count)),
        ],
        compiler_params=pltpu.CompilerParams(
            collective_id=0, has_side_effects=True, vmem_limit_bytes=60 * 2**20
        ),
    )(
        view_factors,
        direct_coeff,
        material.reshape(-1, LANES),
        albedo,
        sky_matrix,
        place.reshape(-1, LANES),
    )


def solution(mesh):
    count, parts = mesh.shape["col"], mesh.shape["parts"]
    cores = 2 if count % 2 == 0 else 1
    side = 2 if parts <= 2 and count % (2 * cores) == 0 else 1
    dims = (count // (side * cores), side, cores)
    return jax.shard_map(
        functools.partial(shards, dims),
        mesh=mesh,
        in_specs=(
            P(("parts", "col"), None),
            P(("parts", "col"), None),
            P(("parts", "col")),
            P("parts"),
            P("col", None),
            P(),
        ),
        out_specs=P(("parts", "col"), None),
        check_vma=False,
    )
```

time: 102 us -> 31.9 us (0.31)
  waiting for transfers between devices: 36.9 us -> 0 us
  Pallas kernels: 0 us -> 30.2 us
  blocking collectives: 26.5 us -> 0 us
  between operations: 13.5 us -> 0.01 us
  matrix products: 8.78 us -> 0 us
  local copies, waits for them, and re-layouts: 9.05 us -> 1.47 us
  other arithmetic: 6.73 us -> 0 us
    all_gather x1 -> x0, waiting for transfers between devices: 36.9 us -> none  [shards(): lax.all_gather(own_reflected, 'col', axis=0, tiled=True)]
    pallas_call x0 -> x1, Pallas kernels: none -> 30.2 us  [shards(): pl.pallas_call(functools.partial(kernel, dims), out_shape=jax.ShapeDtypeS...]
    all_gather x1 -> x0, blocking collectives: 26.5 us -> none  [shards(): piece = lax.all_gather(sky_matrix, 'col', axis=0, tiled=True)]
    dot_general x4 -> x0, matrix products: 8.78 us -> none  [the longest x1 3.06 us: shards(): jnp.dot(reflected, piece, preferred_element_type=jnp.float32)]
    gather x1 -> x0, local copies, waits for them, and re-layouts: 7.43 us -> none  [shards(): direct_sorted = jnp.take(direct_coeff, inverse, axis=1)]
    sort x1 -> x0, other arithmetic: 6.62 us -> none  [shards(): inverse = jnp.argsort(sky_order)]
  transfers between devices with their start and end apart: 1 -> 0, of which waited for: 1 -> 0; matrix products, arithmetic and copies ran while one was open for 2% -> 0% of each run, Pallas kernels for 0% -> 0%
where the time goes in v1:
time: 31.9 us; the launch traced here: 31.7 us
  Pallas kernels  30.2 us (95%)
  local copies, waits for them, and re-layouts  1.47 us (5%)
    pallas_call x1, Pallas kernels, shards(): pl.pallas_call(functools.partial(kernel, dims), out_shape=jax.ShapeDtypeS...  30.2 us
    unnamed x1, local copies, waits for them, and re-layouts  1.47 us

profile of v1, /device:TPU:0, one launch (start us, length us, event | category | flops | bytes accessed | tf_op | source)
XLA Modules:
  0.0 31.7 jit_solution(5275233869358644512)
XLA Ops:
  0.0 30.2 %shard_map.64 = bf16[256,128]{1,0:T(8,128)(2,1)} custom-call(bf16[256,4096]{1,0:T(8,128)(2,1)} %view_hbm.1, bf16[256,2304]{1,0:T(8,128)(2,1)} %direct_hbm.1, s32[2,128]{1,0:T(2,128)} %bitcast.3, f32[16]{0:T(128)} %albedo_ref.1, bf16[144,128]{1,0:T(8,128)(2,1)} %sky_hbm.1, s32[18,128]{1,0:T(8,128)} %bitcast.2), custom_call_target="tpu_custom_call" | custom-call | tf_op jit(solution)/shard_map/pallas_call | solution.py:208
  30.2 1.5 %copy.8 = bf16[256,128]{1,0:T(8,128)(2,1)} copy(bf16[256,128]{1,0:T(8,128)(2,1)} %shard_map.64) | data formatting | bytes 131072

commit v2 on v1

--- a/solution.py
+++ b/solution.py
@@ -10,6 +10,7 @@
 MESH = pl.DeviceIdType.MESH
 LANES = 128
 WIDE = 256
+STAGES = (9,)
 BF16 = jnp.bfloat16
 F32 = jnp.float32
 
@@ -31,10 +32,10 @@
     dims,
     view_hbm,
     direct_hbm,
-    material_ref,
-    albedo_ref,
+    material_hbm,
+    albedo_hbm,
     sky_hbm,
-    place_ref,
+    place_hbm,
     out_ref,
     view_ref,
     direct_ref,
@@ -45,6 +46,9 @@
     reflectance_ref,
     sorted_ref,
     reflected_ref,
+    material_ref,
+    albedo_ref,
+    place_ref,
     load_sem,
     send_sem,
     recv_sem,
@@ -72,14 +76,21 @@
     load_sky = pltpu.make_async_copy(sky_hbm, own_sky, load_sem.at[0])
     load_direct = pltpu.make_async_copy(direct_hbm, direct_ref, load_sem.at[1])
     load_view = pltpu.make_async_copy(view_hbm, view_ref, load_sem.at[2])
+    barrier = pltpu.get_barrier_semaphore()
+    for p in partners:
+        pl.semaphore_signal(barrier, inc=1, device_id={"col": p}, device_id_type=MESH)
+
+    load_place = pltpu.make_async_copy(place_hbm, place_ref, load_sem.at[3])
+    load_material = pltpu.make_async_copy(material_hbm, material_ref, load_sem.at[4])
+    load_albedo = pltpu.make_async_copy(albedo_hbm, albedo_ref, load_sem.at[5])
+    load_place.start()
+    load_material.start()
+    load_albedo.start()
     load_sky.start()
     load_direct.start()
     load_view.start()
 
-    barrier = pltpu.get_barrier_semaphore()
-    for p in partners:
-        pl.semaphore_signal(barrier, inc=1, device_id={"col": p}, device_id_type=MESH)
-
+    load_place.wait()
     lane = lax.broadcasted_iota(jnp.int32, (LANES, LANES), 1)
     for b in range(place_ref.shape[0]):
         spot = jnp.broadcast_to(place_ref[b : b + 1, :], (LANES, LANES)).T
@@ -87,12 +98,32 @@
         low_ref[b * LANES : (b + 1) * LANES, :] = low.astype(BF16)
         high = lax.shift_right_logical(spot, LANES.bit_length() - 1)
         high_ref[b * LANES : (b + 1) * LANES, :] = high.astype(F32).astype(BF16)
+    load_material.wait()
+    load_albedo.wait()
     for b in range(material_ref.shape[0]):
         kind = jnp.broadcast_to(material_ref[b : b + 1, :], (LANES, LANES)).T
         value = jnp.zeros((LANES, LANES), F32)
         for m in range(albedo_ref.shape[0]):
             value = jnp.where(kind == m, albedo_ref[m], value)
         reflectance_ref[b * LANES : (b + 1) * LANES, :] = value
+
+    groups = sorted_ref.shape[1] // WIDE
+    done = [0]
+
+    def sort_columns(group):
+        start = pl.multiple_of(group * WIDE, WIDE)
+        halves = []
+        for half in range(WIDE // LANES):
+            number = (group * (WIDE // LANES) + half).astype(F32).astype(BF16)
+            halves.append(jnp.where(high_ref[...] == number, low_ref[...], jnp.zeros((), BF16)))
+        chosen = jnp.concatenate(halves, axis=1)
+        values = jnp.dot(direct_ref[...], chosen, preferred_element_type=F32)
+        sorted_ref[:, pl.ds(start, WIDE)] = values.astype(BF16)
+        scale = jnp.concatenate([reflectance_ref[...]] * (WIDE // LANES), axis=1)
+        reflected_ref[:, pl.ds(start, WIDE)] = (scale * values).astype(BF16)
+
+    def sort_range(first, last):
+        lax.fori_loop(first, last, lambda g, _: (sort_columns(g), 0)[1], 0)
 
     load_sky.wait()
     pl.semaphore_wait(barrier, len(partners))
@@ -120,7 +151,7 @@
         route = iter(range(2 * nz * ny * nc))
         if across is not None:
             send(phase, everyone, block, me, across, next(route))
-        for p in reversed(line):
+        for p in line:
             send(phase, everyone, block, me, p, next(route))
         if twin is not None:
             send(phase, everyone, block, me, twin, next(route))
@@ -146,28 +177,15 @@
                 arrived(phase, everyone, block, owner)
                 work(owner)
 
-    groups = sorted_ref.shape[1] // WIDE
-    done = [False]
-
-    def sort_columns(group):
-        start = pl.multiple_of(group * WIDE, WIDE)
-        halves = []
-        for half in range(WIDE // LANES):
-            number = (group * (WIDE // LANES) + half).astype(F32).astype(BF16)
-            halves.append(jnp.where(high_ref[...] == number, low_ref[...], jnp.zeros((), BF16)))
-        chosen = jnp.concatenate(halves, axis=1)
-        values = jnp.dot(direct_ref[...], chosen, preferred_element_type=F32)
-        sorted_ref[:, pl.ds(start, WIDE)] = values.astype(BF16)
-        scale = jnp.concatenate([reflectance_ref[...]] * (WIDE // LANES), axis=1)
-        reflected_ref[:, pl.ds(start, WIDE)] = (scale * values).astype(BF16)
-
-    def sort_all(owner):
-        if not done[0]:
-            done[0] = True
+    def sort_some(owner):
+        step = done[0]
+        if step == 0:
             load_direct.wait()
-            lax.fori_loop(0, groups, lambda g, _: (sort_columns(g), 0)[1], 0)
-
-    gather(0, sky_all, sky_rows, sort_all)
+        if step < len(STAGES):
+            sort_range(groups * (STAGES[step - 1] if step else 0) // 9, groups * STAGES[step] // 9)
+        done[0] = step + 1
+
+    gather(0, sky_all, sky_rows, sort_some)
 
     own_hours = pl.ds(pl.multiple_of(me * rows, 16), rows)
     hours_all[own_hours, :] = jnp.dot(reflected_ref[...], sky_all[...], preferred_element_type=F32).astype(BF16)
@@ -202,13 +220,12 @@
     width = -(-count * padded // WIDE) * WIDE
     assert width == count * padded and sky % LANES == 0
     routes = 2 * count
-    any_spec = pl.BlockSpec(memory_space=pl.ANY)
+    hbm = pl.BlockSpec(memory_space=pltpu.HBM)
     vmem = pl.BlockSpec(memory_space=pltpu.VMEM)
-    smem = pl.BlockSpec(memory_space=pltpu.SMEM)
     return pl.pallas_call(
         functools.partial(kernel, dims),
         out_shape=jax.ShapeDtypeStruct((rows, hours), BF16),
-        in_specs=[any_spec, any_spec, vmem, smem, any_spec, vmem],
+        in_specs=[hbm] * 6,
         out_specs=vmem,
         scratch_shapes=[
             pltpu.VMEM((rows, patches), BF16),
@@ -220,7 +237,10 @@
             pltpu.VMEM((rows, LANES), F32),
             pltpu.VMEM((rows, width), BF16),
             pltpu.VMEM((rows, width), BF16),
-            pltpu.SemaphoreType.DMA((3,)),
+            pltpu.VMEM((rows // LANES, LANES), jnp.int32),
+            pltpu.SMEM(albedo.shape, F32),
+            pltpu.VMEM((sky // LANES, LANES), jnp.int32),
+            pltpu.SemaphoreType.DMA((6,)),
             pltpu.SemaphoreType.DMA((2, routes)),
             pltpu.SemaphoreType.DMA((2, count)),
         ],

time: 31.9 us -> 29.8 us (0.934)
  Pallas kernels: 30.2 us -> 28.2 us
    pallas_call x1, Pallas kernels: 30.2 us -> 28.2 us  [shards(): pl.pallas_call(functools.partial(kernel, dims), out_shape=jax.ShapeDtypeS...]
where the time goes in v2:
time: 29.8 us; the launch traced here: 29.6 us
  Pallas kernels  28.2 us (95%)
  local copies, waits for them, and re-layouts  1.47 us (5%)
    pallas_call x1, Pallas kernels, shards(): pl.pallas_call(functools.partial(kernel, dims), out_shape=jax.ShapeDtypeS...  28.2 us
    unnamed x1, local copies, waits for them, and re-layouts  1.47 us

profile of v2, /device:TPU:0, one launch (start us, length us, event | category | flops | bytes accessed | tf_op | source)
XLA Modules:
  0.0 29.6 jit_solution(3156127636942182459)
XLA Ops:
  0.0 28.2 %shard_map.64 = bf16[256,128]{1,0:T(8,128)(2,1)} custom-call(bf16[256,4096]{1,0:T(8,128)(2,1)} %view_hbm.1, bf16[256,2304]{1,0:T(8,128)(2,1)} %direct_hbm.1, s32[2,128]{1,0:T(2,128)} %bitcast.3, f32[16]{0:T(128)} %albedo_hbm.1, bf16[144,128]{1,0:T(8,128)(2,1)} %sky_hbm.1, s32[18,128]{1,0:T(8,128)} %bitcast.2), custom_call_target="tpu_custom_call" | custom-call | tf_op jit(solution)/shard_map/pallas_call | solution.py:225
  28.2 1.5 %copy.8 = bf16[256,128]{1,0:T(8,128)(2,1)} copy(bf16[256,128]{1,0:T(8,128)(2,1)} %shard_map.64) | data formatting | bytes 131072
